TPU v7x, 256 devices: a whole 4x4x8 slice. The times are simulated.
256 devices in a mesh: dp: 32 (over y, z), vocab: 8 (over x, core).
Axes of the slice: x: 4, y: 4, z: 8, core: 2. Of those that a mesh axis runs over, the one named last changes fastest.
Arguments:
- hidden: bfloat16 [24576, 2048], P('dp', 'vocab')
- gain: bfloat16 [2048], replicated, may hold values from 0.5 to 1.5
- head: bfloat16 [2048, 32000], P('dp', 'vocab')
- target_ids: int32 [24576], P('dp'), may hold values from 0 to 31999
- seq_lens: int32 [64], replicated, may hold values from 64 to 704, as said below
- seq_owner: int32 [64], replicated, may hold values from 0 to 31, as said below
Outputs:
- logprob: float32 [24576], P('dp')
- entropy: float32 [24576], P('dp')
Inputs may be any that keep to these rules, and one draw needn't show every extreme that they name: `seq_lens`: the lengths of the sequences owned by one dp index sum to at most 768; in every draw the sequences of some dp index sum to exactly 768. `seq_owner`: every dp index owns exactly 2 sequences.
All inputs are finite; a program needn't handle non-finite values.
Results may differ from a plain program's by a relative error of at most 0.0075.
Values may be sent and summed in bfloat16 or wider, within the bound.
A program may use at most 64 MiB of HBM per device.

v0:
```python
import jax
import jax.numpy as jnp
from jax import lax
from jax.sharding import PartitionSpec as P

EPS = 1e-05


def chunk_bounds(breadth, parts):
    step = -(-breadth // parts)
    step = -(-step // 128) * 128
    bounds = []
    start = 0
    while start < breadth:
        stop = min(start + step, breadth)
        bounds.append((start, stop))
        start = stop
    return bounds


def chunk_stats(normed, columns, local_id, start):
    logits = jnp.dot(normed, columns, preferred_element_type=jnp.float32)
    top = jnp.max(logits, axis=1)
    expo = jnp.exp(logits - top[:, None])
    total = jnp.sum(expo, axis=1)
    weighted = jnp.sum(expo * logits, axis=1)
    ids = start + lax.broadcasted_iota(jnp.int32, logits.shape, 1)
    picked = jnp.sum(jnp.where(ids == local_id[:, None], logits, 0.0), axis=1)
    return (top, total, weighted, picked)


def local(hidden, gain, head, target_ids, seq_lens, seq_owner):
    groups = lax.axis_size("dp")
    position = lax.axis_index("dp")
    slice_index = lax.axis_index("vocab")
    slots = hidden.shape[0]
    breadth = head.shape[1]
    owners = jnp.arange(groups, dtype=jnp.int32)
    loads = jnp.sum(jnp.where(seq_owner[:, None] == owners[None, :], seq_lens[:, None], 0), axis=0)
    own_live = jnp.arange(slots, dtype=jnp.int32) < loads[position]
    features = lax.all_gather(hidden, "vocab", axis=1, tiled=True)
    wide = features.astype(jnp.float32)
    normed = (
        wide
        * lax.rsqrt(jnp.mean(wide * wide, axis=1, keepdims=True) + EPS)
        * gain.astype(jnp.float32)
    ).astype(jnp.bfloat16)
    local_id = target_ids - slice_index * breadth
    parts = []
    for start, stop in chunk_bounds(breadth, 4):
        columns = lax.all_gather(head[:, start:stop], "dp", axis=0, tiled=True)
        parts.append(chunk_stats(normed, columns, local_id, start))
    tops = jnp.stack([p[0] for p in parts])
    top_local = jnp.max(tops, axis=0)
    scale = jnp.exp(tops - top_local[None, :])
    total_local = jnp.sum(jnp.stack([p[1] for p in parts]) * scale, axis=0)
    weighted_local = jnp.sum(jnp.stack([p[2] for p in parts]) * scale, axis=0)
    picked_local = jnp.sum(jnp.stack([p[3] for p in parts]), axis=0)
    top = lax.pmax(top_local, "vocab")
    factor = jnp.exp(top_local - top)
    total, weighted, picked = lax.psum(
        (total_local * factor, weighted_local * factor, picked_local), "vocab"
    )
    lse = top + jnp.log(total)
    logprob = picked - lse
    entropy = lse - weighted / total
    return (jnp.where(own_live, logprob, 0.0), jnp.where(own_live, entropy, 0.0))


def solution(mesh):
    return jax.shard_map(
        local,
        mesh=mesh,
        in_specs=(P("dp", "vocab"), P(), P("dp", "vocab"), P("dp"), P(), P()),
        out_specs=(P("dp"), P("dp")),
        check_vma=False,
    )
```

profile of v0, /device:TPU:32, one launch (start us, length us, event | category | flops | bytes accessed | tf_op | source)
XLA Modules:
  0.0 432.0 jit_solution(7421292452426967437)
XLA Ops:
  7.2 0.0 all-gather.6.cloned.1.call-start
  7.2 0.7 all-gather.6.cloned.1.call-update
  7.9 0.0 all-gather.14.cloned.1.call-start
  7.9 1.6 slice.15
  9.5 0.0 all-gather.14.cloned.1.call-update
  9.5 0.0 all-gather.8.cloned.1.call-start
  9.6 1.8 fusion.20
  11.4 0.0 all-gather.8.cloned.1.call-update
  11.4 0.0 all-gather.10.cloned.1.call-start
  11.5 0.5 all-gather.10.cloned.1.call-update
  12.0 0.0 all-gather.12.cloned.1.call-start
  12.0 0.5 all-gather.12.cloned.1.call-update
  12.6 0.7 convert_element_type.10
  13.3 0.8 select_reduce_fusion.4
  14.1 0.7 dynamic_slice.3
  14.7 0.7 broadcast_subtract_fusion
  15.4 31.2 %all-gather.6.cloned.1.call-done = bf16[768,2048]{1,0:T(8,128)(2,1)} async-done(((bf16[768,256]{1,0:T(8,128)(2,1)}), bf16[768,2048]{1,0:T(8,128)(2,1)}) %all-gather.6.cloned.1.call-update) | async-done | bytes 3145744 | tf_op jit(solution)/shard_map/all_gather | solution.py:41
  46.6 0.0 copy-start.1
  46.6 2.7 fusion
  49.4 82.9 %all-gather.14.cloned.1.call-done = bf16[2048,928]{1,0:T(8,128)(2,1)} async-done(((bf16[64,928]{1,0:T(8,128)(2,1)}), bf16[2048,928]{1,0:T(8,128)(2,1)}) %all-gather.14.cloned.1.call-update) | async-done | bytes 3801104 | tf_op jit(solution)/shard_map/all_gather | solution.py:51
  132.3 0.0 copy-done.1
  132.3 5.9 %fusion.21 = (f32[768]{0:T(1024)S(1)}, f32[768,928]{0,1:T(8,128)S(1)}) fusion(bf16[2048,928]{1,0:T(8,128)(2,1)} %all-gather.14.cloned.1.call-done, bf16[768,2048]{1,0:T(8,128)(2,1)S(1)} %copy-done.1, f32[2048]{0:T(1024)S(1)} %convert_element_type.10, f32[768]{0:T(1024)S(1)} %add_rsqrt_fusion), kind=kOutput, calls=%fused_computation.49 | convolution fusion | flops 2926238976 | bytes 9811968 | tf_op jit(solution)/shard_map/dot_general | solution.py:22
  138.2 0.9 multiply_reduce_fusion.3
  139.0 74.9 %all-gather.8.cloned.1.call-done = bf16[2048,1024]{1,0:T(8,128)(2,1)} async-done(((bf16[64,1024]{1,0:T(8,128)(2,1)}), bf16[2048,1024]{1,0:T(8,128)(2,1)}) %all-gather.8.cloned.1.call-update) | async-done | bytes 4194320 | tf_op jit(solution)/shard_map/all_gather | solution.py:51
  214.0 6.4 %fusion.24 = (f32[768]{0:T(1024)S(1)}, f32[768,1024]{1,0:T(8,128)S(1)}) fusion(bf16[2048,1024]{1,0:T(8,128)(2,1)} %all-gather.8.cloned.1.call-done, bf16[768,2048]{1,0:T(8,128)(2,1)} %all-gather.6.cloned.1.call-done, f32[2048]{0:T(1024)S(1)} %convert_element_type.10, f32[768]{0:T(1024)S(1)} %add_rsqrt_fusion), kind=kOutput, calls=%fused_computation.52 | convolution fusion | flops 3228302592 | bytes 10500096 | tf_op jit(solution)/shard_map/dot_general | solution.py:22
  220.4 75.1 %all-gather.10.cloned.1.call-done = bf16[2048,1024]{1,0:T(8,128)(2,1)} async-done(((bf16[64,1024]{1,0:T(8,128)(2,1)}), bf16[2048,1024]{1,0:T(8,128)(2,1)}) %all-gather.10.cloned.1.call-update) | async-done | bytes 4194320 | tf_op jit(solution)/shard_map/all_gather | solution.py:51
  295.5 8.4 %fusion.22 = (f32[768]{0:T(1024)S(1)}, f32[768,1024]{1,0:T(8,128)}) fusion(bf16[2048,1024]{1,0:T(8,128)(2,1)} %all-gather.10.cloned.1.call-done, bf16[768,2048]{1,0:T(8,128)(2,1)} %all-gather.6.cloned.1.call-done, f32[2048]{0:T(1024)S(1)} %convert_element_type.10, f32[768]{0:T(1024)S(1)} %add_rsqrt_fusion), kind=kOutput, calls=%fused_computation.50 | convolution fusion | flops 3228302592 | bytes 10500096 | tf_op jit(solution)/shard_map/dot_general | solution.py:22
  303.8 73.2 %all-gather.12.cloned.1.call-done = bf16[2048,1024]{1,0:T(8,128)(2,1)} async-done(((bf16[64,1024]{1,0:T(8,128)(2,1)}), bf16[2048,1024]{1,0:T(8,128)(2,1)}) %all-gather.12.cloned.1.call-update) | async-done | bytes 4194320 | tf_op jit(solution)/shard_map/all_gather | solution.py:51
  377.0 0.0 copy-start
  377.0 6.6 %fusion.23 = (f32[768]{0:T(1024)S(1)}, f32[768,1024]{1,0:T(8,128)S(1)}) fusion(bf16[2048,1024]{1,0:T(8,128)(2,1)} %all-gather.12.cloned.1.call-done, bf16[768,2048]{1,0:T(8,128)(2,1)} %all-gather.6.cloned.1.call-done, f32[2048]{0:T(1024)S(1)} %convert_element_type.10, f32[768]{0:T(1024)S(1)} %add_rsqrt_fusion), kind=kOutput, calls=%fused_computation.51 | convolution fusion | flops 3228302592 | bytes 10500096 | tf_op jit(solution)/shard_map/dot_general | solution.py:22
  383.6 0.0 copy-done
  383.6 4.4 %multiply_reduce_fusion.1 = (f32[768]{0:T(1024)S(1)}, f32[768]{0:T(1024)S(1)}, f32[768]{0:T(1024)S(1)}, f32[768]{0:T(1024)S(1)}, f32[768]{0:T(1024)S(1)}, /*inde...) fusion(f32[768,1024]{1,0:T(8,128)S(1)} %copy-done, f32[768]{0:T(1024)S(1)} %get-tuple-element.34, ...), kind=kLoop, calls=%fused_computation.6 | loop fusion | flops 16508160 | bytes 9485312 | tf_op jit(solution)/shard_map/reduce_sum | solution.py:26
  388.1 12.4 %pmax.7 = f32[768]{0:T(1024)S(1)} all-reduce(f32[768]{0:T(1024)S(1)} %maximum_maximum_fusion), channel_id=1, replica_groups=mesh['dp'=32,'vocab'=8] {'vocab'}, use_global_device_ids=true, to_apply=%region_11.12 | all-reduce | flops 768 | bytes 6144 | tf_op jit(solution)/shard_map/pmax | solution.py:59
  400.5 0.1 fusion.9
  400.6 23.6 %all-reduce = (f32[768]{0:T(1024)S(1)}, f32[768]{0:T(1024)S(1)}, f32[768]{0:T(1024)S(1)}) all-reduce(f32[768]{0:T(1024)S(1)} %add_add_fusion, f32[768]{0:T(1024)S(1)} %get-tuple-element.25, f32[768]{0:T(1024)S(1)} %get-tuple-element.24), channel_id=1, replica_groups=mesh['dp'=32,'vocab'=8] {'vocab'}, use_global_device_ids=true, to_apply=%region_6.7 | all-reduce | flops 2304 | bytes 18432 | tf_op jit(solution)/shard_map/psum | solution.py:61
  424.2 1.3 subtract_select_fusion
  (18 shorter events, 0.1 us)
Async XLA Ops:
  7.2 39.5 %all-gather.6.cloned.1.call-start = ((), (), s32[]{:S(2)}) async-start(), calls=%async_computation | async-start | bytes 3538944 | tf_op jit(solution)/shard_map/all_gather | solution.py:41
  7.9 124.4 %all-gather.14.cloned.1.call-start = ((), (), s32[]{:S(2)}) async-start(), calls=%async_computation.4 | async-start | bytes 4325376 | tf_op jit(solution)/shard_map/all_gather | solution.py:51
  9.5 204.4 %all-gather.8.cloned.1.call-start = ((), (), s32[]{:S(2)}) async-start(), calls=%async_computation.1 | async-start | bytes 4325376 | tf_op jit(solution)/shard_map/all_gather | solution.py:51
  11.4 284.1 %all-gather.10.cloned.1.call-start = ((), (), s32[]{:S(2)}) async-start(), calls=%async_computation.2 | async-start | bytes 4325376 | tf_op jit(solution)/shard_map/all_gather | solution.py:51
  12.0 365.0 %all-gather.12.cloned.1.call-start = ((), (), s32[]{:S(2)}) async-start(), calls=%async_computation.3 | async-start | bytes 4325376 | tf_op jit(solution)/shard_map/all_gather | solution.py:51
  46.6 85.6 %copy-start.1 = (bf16[768,2048]{1,0:T(8,128)(2,1)S(1)}, bf16[768,2048]{1,0:T(8,128)(2,1)}, u32[]{:S(2)}) copy-start(bf16[768,2048]{1,0:T(8,128)(2,1)} %all-gather.6.cloned.1.call-done) | copy-start | bytes 9437188
  377.0 6.6 %copy-start = (f32[768,1024]{1,0:T(8,128)S(1)}, f32[768,1024]{1,0:T(8,128)}, u32[]{:S(2)}) copy-start(f32[768,1024]{1,0:T(8,128)} %get-tuple-element.35) | copy-start | bytes 9437188
Sparse Core Ops, SparseCore 0:
  9.8 36.7 all-gather.5
  49.2 83.0 all-gather.13
  134.9 79.0 all-gather.7
  216.4 79.0 all-gather.9
  297.9 79.0 all-gather.11
where the time goes:
time: 432 us
  waiting for transfers between devices  339 us (78%)
  blocking collectives  36 us (8%)
  matrix products  27.2 us (6%)
  between operations  13.9 us (3%)
  other arithmetic  11.6 us (3%)
    all_gather x4, waiting for transfers between devices, local(): columns = lax.all_gather(head[:, start:stop], 'dp', axis=0, tiled=True)  306 us
    all_gather x1, waiting for transfers between devices, local(): features = lax.all_gather(hidden, 'vocab', axis=1, tiled=True)  31.2 us
    dot_general x4, matrix products, chunk_stats(): logits = jnp.dot(normed, columns, preferred_element_type=jnp.float32)  27.2 us
    psum x1, blocking collectives, local(): lax.psum((total_local * factor, weighted_local * factor, picked_local), '...  23.6 us
    pmax x1, blocking collectives, local(): top = lax.pmax(top_local, 'vocab')  12.4 us
  transfers between devices with their start and end apart: 5, of which 5 were waited for; matrix products, arithmetic and copies ran while one was open for 7% of the time, Pallas kernels for 0%

commit v1 on v0

--- a/solution.py
+++ b/solution.py
@@ -4,6 +4,24 @@
 from jax.sharding import PartitionSpec as P
 
 EPS = 1e-05
+
+
+def gather_around(array, axis, dim):
+    ways, here, step = (lax.axis_size(axis), lax.axis_index(axis), array.shape[dim])
+    shape = [n * ways if d == dim else n for d, n in enumerate(array.shape)]
+    full = lax.dynamic_update_slice_in_dim(
+        jnp.zeros(shape, array.dtype), array, here * step, axis=dim
+    )
+    going_up = going_down = array
+    for far in range(1, ways // 2 + 1):
+        going_up = lax.ppermute(going_up, axis, [(d, (d + 1) % ways) for d in range(ways)])
+        full = lax.dynamic_update_slice_in_dim(full, going_up, (here - far) % ways * step, axis=dim)
+        if 2 * far < ways:
+            going_down = lax.ppermute(going_down, axis, [(d, (d - 1) % ways) for d in range(ways)])
+            full = lax.dynamic_update_slice_in_dim(
+                full, going_down, (here + far) % ways * step, axis=dim
+            )
+    return full
 
 
 def chunk_bounds(breadth, parts):
@@ -38,7 +56,7 @@
     owners = jnp.arange(groups, dtype=jnp.int32)
     loads = jnp.sum(jnp.where(seq_owner[:, None] == owners[None, :], seq_lens[:, None], 0), axis=0)
     own_live = jnp.arange(slots, dtype=jnp.int32) < loads[position]
-    features = lax.all_gather(hidden, "vocab", axis=1, tiled=True)
+    features = gather_around(hidden, "vocab", 1)
     wide = features.astype(jnp.float32)
     normed = (
         wide

time: 432 us -> 395 us (0.914)
  waiting for transfers between devices: 339 us -> 290 us
  starting transfers between devices: 0.2 us -> 9 us
  local copies, waits for them, and re-layouts: 4.11 us -> 9.39 us
    all_gather x4, waiting for transfers between devices: 306 us -> 271 us  [local(): columns = lax.all_gather(head[:, start:stop], 'dp', axis=0, tiled=True)]
    all_gather x1 -> x0, waiting for transfers between devices: 31.2 us -> none  [local(): features = lax.all_gather(hidden, 'vocab', axis=1, tiled=True)]
    ppermute x0 -> x7, waiting for transfers between devices: none -> 16.9 us  [the longest x4 16.9 us: gather_around(): lax.ppermute(going_up, axis, [(d, (d + 1) % ways) for d in range(ways)])]
    ppermute x0 -> x7, starting transfers between devices: none -> 8.84 us  [the longest x3 8.81 us: gather_around(): lax.ppermute(going_down, axis, [(d, (d - 1) % ways) for d in range(ways)])]
    dynamic_update_slice x0 -> x8, local copies, waits for them, and re-layouts: none -> 4.35 us  [the longest x4 2.17 us: gather_around(): lax.dynamic_update_slice_in_dim(full, going_up, (here - far) % ways * ste...]
  transfers between devices with their start and end apart: 5 -> 11, of which waited for: 5 -> 8; matrix products, arithmetic and copies ran while one was open for 7% -> 8% of each run, Pallas kernels for 0% -> 0%
where the time goes in v1:
time: 395 us; the launch traced here: 394 us
  waiting for transfers between devices  290 us (73%)
  blocking collectives  36 us (9%)
  matrix products  26.1 us (7%)
  between operations  14 us (4%)
  other arithmetic  10.1 us (3%)
  local copies, waits for them, and re-layouts  9.39 us (2%)
  starting transfers between devices  9 us (2%)
    all_gather x4, waiting for transfers between devices, local(): columns = lax.all_gather(head[:, start:stop], 'dp', axis=0, tiled=True)  271 us
    dot_general x4, matrix products, chunk_stats(): logits = jnp.dot(normed, columns, preferred_element_type=jnp.float32)  26.1 us
    psum x1, blocking collectives, local(): lax.psum((total_local * factor, weighted_local * factor, picked_local), '...  23.6 us
    ppermute x4, waiting for transfers between devices, gather_around(): lax.ppermute(going_up, axis, [(d, (d + 1) % ways) for d in range(ways)])  16.9 us
    pmax x1, blocking collectives, local(): top = lax.pmax(top_local, 'vocab')  12.4 us
    ppermute x3, starting transfers between devices, gather_around(): lax.ppermute(going_down, axis, [(d, (d - 1) % ways) for d in range(ways)])  8.81 us
  transfers between devices with their start and end apart: 11, of which 8 were waited for; matrix products, arithmetic and copies ran while one was open for 8% of the time, Pallas kernels for 0%

profile of v1, /device:TPU:32, one launch (start us, length us, event | category | flops | bytes accessed | tf_op | source)
XLA Modules:
  0.0 394.1 jit_solution(15786374608068407700)
XLA Ops:
  7.2 0.0 copy-start.2
  7.2 0.0 all-gather.11.cloned.1.call-start
  7.2 1.6 slice.15
  8.8 0.0 all-gather.11.cloned.1.call-update
  8.8 0.0 all-gather.9.cloned.1.call-start
  8.9 1.8 fusion.20
  10.7 0.0 all-gather.9.cloned.1.call-update
  10.7 0.0 all-gather.7.cloned.1.call-start
  10.8 0.7 all-gather.7.cloned.1.call-update
  11.5 0.0 all-gather.5.cloned.1.call-start
  11.5 0.5 all-gather.5.cloned.1.call-update
  12.0 0.0 collective-permute-start
  12.1 2.9 collective-permute-start.1
  15.0 5.7 %collective-permute-done = bf16[768,256]{1,0:T(8,128)(2,1)S(1)} collective-permute-done((bf16[768,256]{1,0:T(8,128)(2,1)}, bf16[768,256]{1,0:T(8,128)(2,1)S(1)}, u32[]{:S(2)}, u32[]{:S(2)}) %collective-permute-start) | collective-permute-done | bytes 393248 | tf_op jit(solution)/shard_map/ppermute | solution.py:17
  20.7 0.0 collective-permute-start.2
  20.7 0.8 select_reduce_fusion.4
  21.5 0.7 broadcast_subtract_fusion
  22.2 0.0 collective-permute-done.1
  22.2 2.9 collective-permute-start.3
  25.1 4.1 %collective-permute-done.2 = bf16[768,256]{1,0:T(8,128)(2,1)} collective-permute-done((bf16[768,256]{1,0:T(8,128)(2,1)S(1)}, bf16[768,256]{1,0:T(8,128)(2,1)}, u32[]{:S(2)}, u32[]{:S(2)}) %collective-permute-start.2) | collective-permute-done | bytes 393248 | tf_op jit(solution)/shard_map/ppermute | solution.py:17
  29.2 0.0 collective-permute-start.4
  29.2 1.3 convert_element_type.10
  30.5 0.6 dynamic_slice.3
  31.1 0.4 broadcast_in_dim.46
  31.6 0.5 copy-done.4
  32.2 0.0 collective-permute-done.3
  32.2 3.0 collective-permute-start.5
  35.1 1.0 constant_dynamic-update-slice_fusion.4
  36.2 1.7 collective-permute-done.4
  37.9 1.0 constant_dynamic-update-slice_fusion.3
  39.0 1.0 constant_dynamic-update-slice_fusion.2
  40.0 1.1 constant_dynamic-update-slice_fusion.1
  41.2 5.4 %collective-permute-done.6 = bf16[768,256]{1,0:T(8,128)(2,1)S(1)} collective-permute-done((bf16[768,256]{1,0:T(8,128)(2,1)}, bf16[768,256]{1,0:T(8,128)(2,1)S(1)}, u32[]{:S(2)}, u32[]{:S(2)}) %collective-permute-start.6) | collective-permute-done | bytes 393248 | tf_op jit(solution)/shard_map/ppermute | solution.py:17
  46.6 0.7 fusion
  47.3 47.9 %all-gather.11.cloned.1.call-done = bf16[2048,928]{1,0:T(8,128)(2,1)} async-done(((bf16[64,928]{1,0:T(8,128)(2,1)}), bf16[2048,928]{1,0:T(8,128)(2,1)}) %all-gather.11.cloned.1.call-update) | async-done | bytes 3801104 | tf_op jit(solution)/shard_map/all_gather | solution.py:69
  95.2 5.7 %fusion.21 = (f32[768]{0:T(1024)S(1)}, f32[768,928]{0,1:T(8,128)S(1)}) fusion(bf16[2048,928]{1,0:T(8,128)(2,1)} %all-gather.11.cloned.1.call-done, bf16[768,2048]{1,0:T(8,128)(2,1)S(1)} %constant_dynamic-update-slice_fusion.7, f32[2048]{0:T(1024)S(1)} %copy-done.5, f32[768]{0:T(1024)S(1)} %add_rsqrt_fusion), kind=kOutput, calls=%fused_computation.57 | convolution fusion | flops 2926238976 | bytes 9811968 | tf_op jit(solution)/shard_map/dot_general | solution.py:40
  101.0 0.9 multiply_reduce_fusion.3
  101.9 75.1 %all-gather.9.cloned.1.call-done = bf16[2048,1024]{1,0:T(8,128)(2,1)} async-done(((bf16[64,1024]{1,0:T(8,128)(2,1)}), bf16[2048,1024]{1,0:T(8,128)(2,1)}) %all-gather.9.cloned.1.call-update) | async-done | bytes 4194320 | tf_op jit(solution)/shard_map/all_gather | solution.py:69
  176.9 7.4 %fusion.23 = (f32[768]{0:T(1024)S(1)}, f32[768,1024]{1,0:T(8,128)}) fusion(bf16[2048,1024]{1,0:T(8,128)(2,1)} %all-gather.9.cloned.1.call-done, bf16[768,2048]{1,0:T(8,128)(2,1)S(1)} %constant_dynamic-update-slice_fusion.7, f32[2048]{0:T(1024)S(1)} %copy-done.5, f32[768]{0:T(1024)S(1)} %add_rsqrt_fusion), kind=kOutput, calls=%fused_computation.59 | convolution fusion | flops 3228302592 | bytes 10500096 | tf_op jit(solution)/shard_map/dot_general | solution.py:40
  184.3 74.3 %all-gather.7.cloned.1.call-done = bf16[2048,1024]{1,0:T(8,128)(2,1)} async-done(((bf16[64,1024]{1,0:T(8,128)(2,1)}), bf16[2048,1024]{1,0:T(8,128)(2,1)}) %all-gather.7.cloned.1.call-update) | async-done | bytes 4194320 | tf_op jit(solution)/shard_map/all_gather | solution.py:69
  258.6 7.4 %fusion.22 = (f32[768]{0:T(1024)S(1)}, f32[768,1024]{1,0:T(8,128)}) fusion(bf16[2048,1024]{1,0:T(8,128)(2,1)} %all-gather.7.cloned.1.call-done, bf16[768,2048]{1,0:T(8,128)(2,1)S(1)} %constant_dynamic-update-slice_fusion.7, f32[2048]{0:T(1024)S(1)} %copy-done.5, f32[768]{0:T(1024)S(1)} %add_rsqrt_fusion), kind=kOutput, calls=%fused_computation.58 | convolution fusion | flops 3228302592 | bytes 10500096 | tf_op jit(solution)/shard_map/dot_general | solution.py:40
  266.0 74.1 %all-gather.5.cloned.1.call-done = bf16[2048,1024]{1,0:T(8,128)(2,1)} async-done(((bf16[64,1024]{1,0:T(8,128)(2,1)}), bf16[2048,1024]{1,0:T(8,128)(2,1)}) %all-gather.5.cloned.1.call-update) | async-done | bytes 4194320 | tf_op jit(solution)/shard_map/all_gather | solution.py:69
  340.1 5.6 %fusion.24 = (f32[768]{0:T(1024)S(1)}, f32[768,1024]{1,0:T(8,128)S(1)}) fusion(bf16[2048,1024]{1,0:T(8,128)(2,1)} %all-gather.5.cloned.1.call-done, bf16[768,2048]{1,0:T(8,128)(2,1)S(1)} %constant_dynamic-update-slice_fusion.7, f32[2048]{0:T(1024)S(1)} %copy-done.5, f32[768]{0:T(1024)S(1)} %add_rsqrt_fusion), kind=kOutput, calls=%fused_computation.60 | convolution fusion | flops 3228302592 | bytes 10500096 | tf_op jit(solution)/shard_map/dot_general | solution.py:40
  345.8 4.4 %multiply_reduce_fusion.1 = (f32[768]{0:T(1024)S(1)}, f32[768]{0:T(1024)S(1)}, f32[768]{0:T(1024)S(1)}, f32[768]{0:T(1024)S(1)}, f32[768]{0:T(1024)S(1)}, /*inde...) fusion(f32[768,1024]{1,0:T(8,128)S(1)} %copy-done.1, f32[768]{0:T(1024)S(1)} %get-tuple-element.34, ...), kind=kLoop, calls=%fused_computation.6 | loop fusion | flops 16508160 | bytes 9485312 | tf_op jit(solution)/shard_map/reduce_sum | solution.py:44
  350.2 12.4 %pmax.7 = f32[768]{0:T(1024)S(1)} all-reduce(f32[768]{0:T(1024)S(1)} %maximum_maximum_fusion), channel_id=1, replica_groups=mesh['dp'=32,'vocab'=8] {'vocab'}, use_global_device_ids=true, to_apply=%region_11.12 | all-reduce | flops 768 | bytes 6144 | tf_op jit(solution)/shard_map/pmax | solution.py:77
  362.7 0.1 fusion.9
  362.8 23.6 %all-reduce = (f32[768]{0:T(1024)S(1)}, f32[768]{0:T(1024)S(1)}, f32[768]{0:T(1024)S(1)}) all-reduce(f32[768]{0:T(1024)S(1)} %add_add_fusion, f32[768]{0:T(1024)S(1)} %get-tuple-element.25, f32[768]{0:T(1024)S(1)} %get-tuple-element.24), channel_id=1, replica_groups=mesh['dp'=32,'vocab'=8] {'vocab'}, use_global_device_ids=true, to_apply=%region_6.7 | all-reduce | flops 2304 | bytes 18432 | tf_op jit(solution)/shard_map/psum | solution.py:79
  386.3 1.2 subtract_select_fusion
  (34 shorter events, 0.3 us)
Async XLA Ops:
  7.2 24.4 %copy-start.2 = (bf16[768,256]{1,0:T(8,128)(2,1)S(1)}, bf16[768,256]{1,0:T(8,128)(2,1)}, u32[]{:S(2)}) copy-start(bf16[768,256]{1,0:T(8,128)(2,1)} %param.6) | copy-start | bytes 1179652
  7.2 88.1 %all-gather.11.cloned.1.call-start = ((), (), s32[]{:S(2)}) async-start(), calls=%async_computation.3 | async-start | bytes 4325376 | tf_op jit(solution)/shard_map/all_gather | solution.py:69
  8.8 168.1 %all-gather.9.cloned.1.call-start = ((), (), s32[]{:S(2)}) async-start(), calls=%async_computation.2 | async-start | bytes 4325376 | tf_op jit(solution)/shard_map/all_gather | solution.py:69
  10.7 247.9 %all-gather.7.cloned.1.call-start = ((), (), s32[]{:S(2)}) async-start(), calls=%async_computation.1 | async-start | bytes 4325376 | tf_op jit(solution)/shard_map/all_gather | solution.py:69
  11.5 328.7 %all-gather.5.cloned.1.call-start = ((), (), s32[]{:S(2)}) async-start(), calls=%async_computation | async-start | bytes 4325376 | tf_op jit(solution)/shard_map/all_gather | solution.py:69
  12.0 8.6 %collective-permute-start = (bf16[768,256]{1,0:T(8,128)(2,1)}, bf16[768,256]{1,0:T(8,128)(2,1)S(1)}, u32[]{:S(2)}, u32[]{:S(2)}) collective-permute-start(bf16[768,256]{1,0:T(8,128)(2,1)} %param.6), channel_id=1, source_target_pairs={{0,1},{1,2},{2,3},{3,4},{4,5},{5,6},{6,7},{7,0},{8,9},{9,10},{10,1... | collective-permute-start | bytes 1179656 | tf_op jit(solution)/shard_map/ppermute | solution.py:17
  12.1 10.1 %collective-permute-start.1 = (bf16[768,256]{1,0:T(8,128)(2,1)}, bf16[768,256]{1,0:T(8,128)(2,1)}, u32[]{:S(2)}, u32[]{:S(2)}) collective-permute-start(bf16[768,256]{1,0:T(8,128)(2,1)} %param.6), channel_id=1, source_target_pairs={{0,7},{1,0},{2,1},{3,2},{4,3},{5,4},{6,5},{7,6},{8,15},{9,8},{10,9... | collective-permute-start | bytes 1179656 | tf_op jit(solution)/shard_map/ppermute | solution.py:20
  20.7 9.8 %copy-start.3 = (bf16[768,256]{1,0:T(8,128)(2,1)}, bf16[768,256]{1,0:T(8,128)(2,1)S(1)}, u32[]{:S(2)}) copy-start(bf16[768,256]{1,0:T(8,128)(2,1)S(1)} %collective-permute-done) | copy-start | bytes 1179652
  20.7 8.5 %collective-permute-start.2 = (bf16[768,256]{1,0:T(8,128)(2,1)S(1)}, bf16[768,256]{1,0:T(8,128)(2,1)}, u32[]{:S(2)}, u32[]{:S(2)}) collective-permute-start(bf16[768,256]{1,0:T(8,128)(2,1)S(1)} %collective-permute-done), channel_id=1, source_target_pairs={{0,1},{1,2},{2,3},{3,4},{4,5},{5,6},{6,7},{7,0},{8,9},{9,10},{10,1... | collective-permute-start | bytes 1179656 | tf_op jit(solution)/shard_map/ppermute | solution.py:17
  22.2 10.0 %collective-permute-start.3 = (bf16[768,256]{1,0:T(8,128)(2,1)}, bf16[768,256]{1,0:T(8,128)(2,1)}, u32[]{:S(2)}, u32[]{:S(2)}) collective-permute-start(bf16[768,256]{1,0:T(8,128)(2,1)} %collective-permute-done.1), channel_id=1, source_target_pairs={{0,7},{1,0},{2,1},{3,2},{4,3},{5,4},{6,5},{7,6},{8,15},{9,8},{10,9... | collective-permute-start | bytes 1179656 | tf_op jit(solution)/shard_map/ppermute | solution.py:20
  29.2 8.7 %collective-permute-start.4 = (bf16[768,256]{1,0:T(8,128)(2,1)}, bf16[768,256]{1,0:T(8,128)(2,1)}, u32[]{:S(2)}, u32[]{:S(2)}) collective-permute-start(bf16[768,256]{1,0:T(8,128)(2,1)} %collective-permute-done.2), channel_id=1, source_target_pairs={{0,1},{1,2},{2,3},{3,4},{4,5},{5,6},{6,7},{7,0},{8,9},{9,10},{10,1... | collective-permute-start | bytes 1179656 | tf_op jit(solution)/shard_map/ppermute | solution.py:17
  31.1 1.0 copy-start.4
  32.2 8.9 %collective-permute-start.5 = (bf16[768,256]{1,0:T(8,128)(2,1)}, bf16[768,256]{1,0:T(8,128)(2,1)S(1)}, u32[]{:S(2)}, u32[]{:S(2)}) collective-permute-start(bf16[768,256]{1,0:T(8,128)(2,1)} %collective-permute-done.3), channel_id=1, source_target_pairs={{0,7},{1,0},{2,1},{3,2},{4,3},{5,4},{6,5},{7,6},{8,15},{9,8},{10,9... | collective-permute-start | bytes 1179656 | tf_op jit(solution)/shard_map/ppermute | solution.py:20
  37.9 8.6 %collective-permute-start.6 = (bf16[768,256]{1,0:T(8,128)(2,1)}, bf16[768,256]{1,0:T(8,128)(2,1)S(1)}, u32[]{:S(2)}, u32[]{:S(2)}) collective-permute-start(bf16[768,256]{1,0:T(8,128)(2,1)} %collective-permute-done.4), channel_id=1, source_target_pairs={{0,1},{1,2},{2,3},{3,4},{4,5},{5,6},{6,7},{7,0},{8,9},{9,10},{10,1... | collective-permute-start | bytes 1179656 | tf_op jit(solution)/shard_map/ppermute | solution.py:17
  39.0 56.3 %copy-start.5 = (f32[2048]{0:T(1024)S(1)}, f32[2048]{0:T(1024)}, u32[]{:S(2)}) copy-start(f32[2048]{0:T(1024)} %convert_element_type.10) | copy-start | bytes 24580
  340.1 5.6 %copy-start = (f32[768,1024]{1,0:T(8,128)S(1)}, f32[768,1024]{1,0:T(8,128)}, u32[]{:S(2)}) copy-start(f32[768,1024]{1,0:T(8,128)} %get-tuple-element.37) | copy-start | bytes 9437188
  340.1 5.6 %copy-start.1 = (f32[768,1024]{1,0:T(8,128)S(1)}, f32[768,1024]{1,0:T(8,128)}, u32[]{:S(2)}) copy-start(f32[768,1024]{1,0:T(8,128)} %get-tuple-element.35) | copy-start | bytes 9437188
Sparse Core Ops, SparseCore 0:
  10.6 84.5 all-gather.10
  97.8 79.0 all-gather.8
  179.5 79.0 all-gather.6
  261.0 79.0 all-gather.4
